TPU v7x, 128 devices: a whole 4x4x4 slice. The times are simulated.
128 devices in a mesh: seq: 8 (over y, x_hi), rep: 16 (over x_lo, z, core).
Axes of the slice: x: 4 (x_hi: 2, x_lo: 2; x = x_hi * 2 + x_lo), y: 4, z: 4, core: 2. Of those that a mesh axis runs over, the one named last changes fastest.
Arguments:
- tile_embed: bfloat16 [16, 8192, 768], P('rep', 'seq'), may hold values from -6 to 6
- tile_source: int32 [16, 8192], P('rep', 'seq'), may hold values from 0 to 8191, as said below
- slide_len: int32 [16], P('rep'), may hold values from 4096 to 8192
- grad_out: bfloat16 [16, 8192, 768], P('rep', 'seq'), may hold values from -6 to 6
- w_query: bfloat16 [768, 768], replicated, may hold values from -0.11727427342914273 to 0.11727427342914273
- w_key: bfloat16 [768, 768], replicated, may hold values from -0.11727427342914273 to 0.11727427342914273
- w_value: bfloat16 [768, 768], replicated, may hold values from -0.21875 to 0.21875
- w_out: bfloat16 [768, 768], replicated, may hold values from -0.21875 to 0.21875
Outputs:
- encoded: bfloat16 [16, 8192, 768], P('rep', 'seq')
- embed_grad: bfloat16 [16, 8192, 768], P('rep', 'seq')
- grad_query: float32 [768, 768], replicated
- grad_key: float32 [768, 768], replicated
- grad_value: float32 [768, 768], replicated
- grad_outproj: float32 [768, 768], replicated
Inputs may be any that keep to these rules, and one draw needn't show every extreme that they name: For each slide, tile_source is a permutation of 0 to 8191; each run of 1024 slide positions (aligned) takes exactly 1024 // (number of such runs) rows from each aligned run of 1024 rows of tile_embed.
All inputs are finite; a program needn't handle non-finite values.
Results may differ from a plain program's by a relative error of at most 0.0025.
The roundings to bfloat16 on the way count: a program that leaves them out, or rounds other values in their place, can miss the bound.
Values may be sent and summed in bfloat16 or wider, within the bound.
A program may use at most 192 MiB of HBM per device.

v0:
```python
import jax
import jax.numpy as jnp
from jax import lax
from jax.sharding import PartitionSpec as P

HEADS = 16
SEG = 1024
RATE = 16
NEGATIVE = -1e30


def sent_together(arrays, axis, dim, along):
    both = jnp.concatenate(arrays, axis=along)
    result, at, done = (lax.all_gather(both, axis, axis=dim, tiled=True), 0, [])
    for a in arrays:
        done.append(lax.slice_in_dim(result, at, at + a.shape[along], axis=along))
        at += a.shape[along]
    return tuple(done)


def side_by_side(arrays, axis, dim, along):
    widths = [a.shape[along] for a in arrays]
    both = jnp.concatenate(arrays, axis=along)
    result = lax.psum_scatter(both, axis, scatter_dimension=dim, tiled=True)
    return tuple(jnp.split(result, [sum(widths[:k]) for k in range(1, len(widths))], axis=along))


def chosen(dilation, head_count):
    return jnp.arange(dilation)[:, None] == (jnp.arange(head_count) % dilation)[None, :]


def sparse_rows(dense, dilation):
    row_count, head_count, trailing = dense.shape
    blocks = dense.astype(jnp.float32).reshape(
        row_count // dilation, dilation, head_count, trailing
    )
    selected = chosen(dilation, head_count)[None, :, :, None]
    return jnp.sum(jnp.where(selected, blocks, jnp.float32(0.0)), axis=1)


def spread_rows(sparse, dilation, filler):
    row_count, head_count, trailing = sparse.shape
    selected = chosen(dilation, head_count)[None, :, :, None]
    spread = jnp.where(selected, sparse[:, None], jnp.float32(filler))
    return spread.reshape(row_count * dilation, head_count, trailing)


def product(pattern, left_side, right_side):
    return jnp.einsum(pattern, left_side, right_side, preferred_element_type=jnp.float32)


def masked_scores(queries, key_rows, key_ok, pieces, scaling):
    scores = product("nqd,nkd->nqk", queries, key_rows) * scaling
    return jnp.where(key_ok.reshape(pieces, 1, -1), scores, NEGATIVE)


def head_forward(queries, key_rows, values, key_ok, pieces, scaling):
    head_width = queries.shape[-1]
    queries = queries.reshape(pieces, -1, head_width)
    key_rows = key_rows.reshape(pieces, -1, head_width)
    values = values.reshape(pieces, -1, head_width)
    scores = masked_scores(queries, key_rows, key_ok, pieces, scaling)
    maxima = jnp.max(scores, axis=-1)
    weights = jnp.exp(scores - maxima[..., None])
    totals = jnp.sum(weights, axis=-1)
    numerator = product("nqk,nkd->nqd", weights.astype(jnp.bfloat16), values)
    return (numerator.reshape(-1, head_width), maxima.reshape(-1), totals.reshape(-1))


def split_pieces(arrays, pieces):
    return tuple((member.reshape(pieces, -1, member.shape[-1]) for member in arrays))


def score_terms(queries, key_rows, values, key_ok, log_total, upstream, deltas, pieces, scaling):
    scores = masked_scores(queries, key_rows, key_ok, pieces, scaling)
    probabilities = jnp.exp(scores - log_total.reshape(pieces, -1, 1))
    prob_grad = product("nqd,nkd->nqk", upstream, values)
    score_grad = (probabilities * (prob_grad - deltas.reshape(pieces, -1, 1))).astype(jnp.bfloat16)
    return (probabilities, score_grad)


def head_backward(queries, key_rows, values, key_ok, log_total, upstream, deltas, pieces, scaling):
    head_width = queries.shape[-1]
    queries, key_rows, values, upstream = split_pieces(
        (queries, key_rows, values, upstream), pieces
    )
    probabilities, score_grad = score_terms(
        queries, key_rows, values, key_ok, log_total, upstream, deltas, pieces, scaling
    )
    value_grad = product("nqk,nqd->nkd", probabilities.astype(jnp.bfloat16), upstream)
    query_grad = product("nqk,nkd->nqd", score_grad, key_rows) * scaling
    key_grad = product("nqk,nqd->nkd", score_grad, queries) * scaling
    return (
        query_grad.reshape(-1, head_width),
        key_grad.reshape(-1, head_width),
        value_grad.reshape(-1, head_width),
    )


def heads_map(function, arrays, pieces, scaling):
    transposed = tuple((jnp.moveaxis(member, 1, 0) for member in arrays))
    results = lax.map(lambda members: function(*members, pieces, scaling), transposed)
    return tuple((jnp.moveaxis(member, 0, 1) for member in results))


def merge_parts(local_part, remote, dilation):
    numer_local, max_local, total_local = local_part
    numer_far = spread_rows(remote[0], dilation, 0.0)
    max_far = spread_rows(remote[1][..., None], dilation, NEGATIVE)[..., 0]
    total_far = spread_rows(remote[2][..., None], dilation, 0.0)[..., 0]
    highest = jnp.maximum(max_local, max_far)
    weight_local = jnp.exp(max_local - highest)
    weight_far = jnp.exp(max_far - highest)
    combined = total_local * weight_local + total_far * weight_far
    output = (numer_local * weight_local[..., None] + numer_far * weight_far[..., None]) / combined[
        ..., None
    ]
    return (output, highest + jnp.log(combined))


def project(left_side, right_side):
    return jnp.dot(left_side, right_side, preferred_element_type=jnp.float32)


def per_device(tile_embed, tile_source, slide_len, grad_out, w_query, w_key, w_value, w_out):
    owned_rows = tile_embed[0]
    source = tile_source[0]
    row_count, features = owned_rows.shape
    stripes = lax.axis_size("seq")
    stripe = lax.axis_index("seq")
    portion = row_count // stripes
    owner_dev = source // row_count
    ordering = jnp.argsort(owner_dev, stable=True)
    wanted = (source % row_count)[ordering].reshape(stripes, portion)
    requested = lax.all_to_all(wanted, "seq", split_axis=0, concat_axis=0, tiled=True)
    picked = jnp.take(owned_rows, requested.reshape(-1), axis=0).reshape(stripes, portion, features)
    arrived = lax.all_to_all(picked, "seq", split_axis=0, concat_axis=0, tiled=True).reshape(
        row_count, features
    )
    embedded = jnp.zeros_like(arrived).at[ordering].set(arrived)
    length = slide_len[0]
    upstream_in = grad_out[0]
    head_dim = features // HEADS
    scaling = head_dim ** (-0.5)
    positions = stripe * row_count + jnp.arange(row_count)
    valid_rows = positions < length
    queries = project(embedded, w_query).astype(jnp.bfloat16).reshape(row_count, HEADS, head_dim)
    key_rows = project(embedded, w_key).astype(jnp.bfloat16).reshape(row_count, HEADS, head_dim)
    values = project(embedded, w_value).astype(jnp.bfloat16).reshape(row_count, HEADS, head_dim)
    local_ok = jnp.broadcast_to(valid_rows[:, None], (row_count, HEADS))
    local_part = heads_map(
        head_forward, (queries, key_rows, values, local_ok), row_count // SEG, scaling
    )
    sparse_q = sparse_rows(queries, RATE).astype(jnp.bfloat16)
    sparse_k = sparse_rows(key_rows, RATE).astype(jnp.bfloat16)
    sparse_v = sparse_rows(values, RATE).astype(jnp.bfloat16)
    near_count = sparse_k.shape[0]
    far_k, far_v = sent_together(
        (sparse_k.reshape(near_count, features), sparse_v.reshape(near_count, features)),
        "seq",
        0,
        1,
    )
    far_count = far_k.shape[0]
    far_k = far_k.reshape(far_count, HEADS, head_dim)
    far_v = far_v.reshape(far_count, HEADS, head_dim)
    sparse_pos = jnp.arange(far_count)[:, None] * RATE + (jnp.arange(HEADS) % RATE)[None, :]
    sparse_ok = sparse_pos < length
    remote = heads_map(head_forward, (sparse_q, far_k, far_v, sparse_ok), 1, scaling)
    output, log_total = merge_parts(local_part, remote, RATE)
    attended = (
        (output * valid_rows[:, None, None]).astype(jnp.bfloat16).reshape(row_count, features)
    )
    encoded = (embedded.astype(jnp.float32) + project(attended, w_out)).astype(jnp.bfloat16)
    upstream = (
        (project(upstream_in, w_out.T) * valid_rows[:, None])
        .astype(jnp.bfloat16)
        .reshape(row_count, HEADS, head_dim)
    )
    deltas = jnp.sum(upstream.astype(jnp.float32) * output, axis=-1)
    grad_outproj = jnp.einsum(
        "td,te->de", attended, upstream_in, preferred_element_type=jnp.float32
    )
    local_grads = heads_map(
        head_backward,
        (queries, key_rows, values, local_ok, log_total, upstream, deltas),
        row_count // SEG,
        scaling,
    )
    sparse_up = sparse_rows(upstream, RATE).astype(jnp.bfloat16)
    sparse_delta = sparse_rows(deltas[..., None], RATE)[..., 0]
    sparse_total = sparse_rows(log_total[..., None], RATE)[..., 0]
    remote_grads = heads_map(
        head_backward,
        (sparse_q, far_k, far_v, sparse_ok, sparse_total, sparse_up, sparse_delta),
        1,
        scaling,
    )
    key_back, value_back = side_by_side(
        (
            remote_grads[1].reshape(far_count, features),
            remote_grads[2].reshape(far_count, features),
        ),
        "seq",
        0,
        1,
    )
    key_back = key_back.reshape(near_count, HEADS, head_dim)
    value_back = value_back.reshape(near_count, HEADS, head_dim)
    query_far = remote_grads[0]
    query_grad = (
        (local_grads[0] + spread_rows(query_far, RATE, 0.0))
        .astype(jnp.bfloat16)
        .reshape(row_count, features)
    )
    key_grad = (
        (local_grads[1] + spread_rows(key_back, RATE, 0.0))
        .astype(jnp.bfloat16)
        .reshape(row_count, features)
    )
    value_grad = (
        (local_grads[2] + spread_rows(value_back, RATE, 0.0))
        .astype(jnp.bfloat16)
        .reshape(row_count, features)
    )
    embed_grad = upstream_in.astype(jnp.float32) + project(query_grad, w_query.T)
    embed_grad = embed_grad + project(key_grad, w_key.T)
    embed_grad = (embed_grad + project(value_grad, w_value.T)).astype(jnp.bfloat16)
    grad_query = jnp.einsum("td,te->de", embedded, query_grad, preferred_element_type=jnp.float32)
    grad_key = jnp.einsum("td,te->de", embedded, key_grad, preferred_element_type=jnp.float32)
    grad_value = jnp.einsum("td,te->de", embedded, value_grad, preferred_element_type=jnp.float32)
    summed = lax.psum((grad_query, grad_key, grad_value, grad_outproj), ("seq", "rep"))
    return (encoded[None], embed_grad[None], summed[0], summed[1], summed[2], summed[3])


def solution(mesh):
    return jax.shard_map(
        per_device,
        mesh=mesh,
        in_specs=(
            P("rep", "seq", None),
            P("rep", "seq"),
            P("rep"),
            P("rep", "seq", None),
            P(),
            P(),
            P(),
            P(),
        ),
        out_specs=(P("rep", "seq", None), P("rep", "seq", None), P(), P(), P(), P()),
        check_vma=False,
    )
```

profile of v0, /device:TPU:1, one launch (start us, length us, event | category | flops | bytes accessed | tf_op | source)
XLA Modules:
  0.0 927.7 jit_solution(13894790200978015584)
XLA Ops:
  8.0 4.4 sort.17
  12.4 4.5 gather_fusion
  16.9 13.8 %all_to_all.14 = s32[8,1,128]{2,1,0:T(1,128)S(1)} all-to-all(s32[8,1,128]{2,1,0:T(1,128)S(1)} %bitcast.386), channel_id=1, replica_groups=mesh['seq'=8,'rep'=16] {'seq'}, dimensions={0} | all-to-all | bytes 8192 | tf_op jit(solution)/shard_map/all_to_all | solution.py:135
  30.7 4.0 gather_fusion.1
  36.1 4.4 all-to-all-start.1
  42.5 2.7 multiply_convert_fusion.2
  47.3 4.8 copy.100
  52.1 3.1 copy.99
  55.3 7.8 reshape.434
  65.1 6.4 scatter_custom_fusion
  71.5 3.3 convolution_convert_fusion.2
  76.8 7.8 reshape.431
  84.6 3.2 convolution_convert_fusion.1
  90.0 7.8 reshape.432
  97.8 4.3 convolution_convert_fusion
  102.1 3.1 copy.87
  105.1 7.8 reshape.433
  112.9 14.1 %select_reduce_fusion = (bf16[64,16,48]{2,1,0:T(8,128)(2,1)S(1)}, bf16[64,16,48]{2,1,0:T(8,128)(2,1)}, bf16[64,16,48]{2,1,0:T(8,128)(2,1)}, bf16[64,16,48]{2,1,0:T(8,128)(2,1)}) fusion(f32[64,16,16,48]{3,2,1,0:T(8,128)} %reshape.434, pred[16,16]{1,0:T(8,128)(4,1)} %copy-done.23, f32[64,16,16,48]{3,2,1,0:T(8,128)} %reshape.432, ...), kind=kLoop, calls=%fused_computation.133 | loop fusion | flops 6094848 | bytes 12976384 | tf_op jit(solution)/shard_map/reduce_sum | solution.py:38
  132.7 3.2 copy.80
  135.9 3.2 copy.81
  139.0 3.2 copy.82
  144.3 142.6 %while.56 = (s32[]{:T(128)}, f32[16,1024,48]{1,2,0:T(8,128)}, f32[16,1024]{1,0:T(8,128)S(1)}, f32[16,1024]{1,0:T(8,128)S(1)}, pred[16,1024]{1,0:T(8,128)(4,1)S(1...) while((s32[]{:T(128)}, f32[16,1024,48]{1,2,0:T(8,128)}, ...), condition=%wide.region_5.6_spmd, body=%wide.region_2.5_spmd.sunk | while | flops 212858880 | bytes 30383244 | solution.py:102
  149.1 4.0 fusion.204
  158.0 4.0 fusion.204
  166.9 4.2 fusion.204
  176.0 4.0 fusion.204
  184.9 4.0 fusion.204
  193.8 4.0 fusion.204
  202.7 4.0 fusion.204
  211.6 4.0 fusion.204
  220.5 4.0 fusion.204
  229.5 4.0 fusion.204
  238.4 4.0 fusion.204
  247.2 4.0 fusion.204
  256.1 4.0 fusion.204
  265.0 4.0 fusion.204
  273.9 4.0 fusion.204
  282.8 4.0 fusion.204
  287.0 7.9 copy.83
  301.3 42.2 %while.57 = (s32[]{:T(128)}, f32[16,64,48]{1,2,0:T(8,128)S(1)}, f32[16,64]{1,0:T(8,128)S(1)}, f32[16,64]{1,0:T(8,128)S(1)}, pred[16,512]{1,0:T(8,128)(4,1)S(1)},...) while((s32[]{:T(128)}, f32[16,64,48]{1,2,0:T(8,128)S(1)}, ...), condition=%wide.region_12.13_spmd, body=%wide.region_9.12_spmd.sunk | while | flops 6520706 | bytes 702321 | solution.py:102
  346.2 13.4 %multiply_convert_fusion.1 = (bf16[1024,16,48]{2,1,0:T(8,128)(2,1)}, f32[1024,16,48]{2,1,0:T(8,128)S(1)}) fusion(f32[1024]{0:T(1024)S(1)} %copy-done.25, f32[1024,16]{1,0:T(8,128)} %copy.97, f32[1024,16]{1,0:T(8,128)S(1)} %copy.96, f32[64,16,48]{2,1,0:T(8,128)S(1)} %copy.95, pred[1024,16]{1,0:T(8,128)(4,1)S(1)} %copy.94, f32[1024,16]{1,0:T(8,128)S(1)} %copy.93, ...), kind=kLoop, calls=%fused_computation.135 | loop fusion | flops 5505024 | bytes 8278016 | tf_op jit(solution)/shard_map/convert_element_type | solution.py:172
  362.9 103.9 %while.59 = (s32[]{:T(128)}, f32[16,64,48]{1,2,0:T(8,128)S(1)}, f32[16,512,48]{1,2,0:T(8,128)}, f32[16,512,48]{1,2,0:T(8,128)}, pred[16,512]{1,0:T(8,128)(4,1)S(...) while((s32[]{:T(128)}, f32[16,64,48]{1,2,0:T(8,128)S(1)}, ...), condition=%wide.region_20.21_spmd, body=%wide.region_19.20_spmd.sunk | while | flops 15985666 | bytes 1278077 | solution.py:102
  466.8 3.9 pad_maximum_fusion
  470.7 3.9 copy.119
  481.0 181.1 %while.58 = (s32[]{:T(128)}, f32[16,1024,48]{1,2,0:T(8,128)}, f32[16,1024,48]{1,2,0:T(8,128)}, f32[16,1024,48]{1,2,0:T(8,128)}, pred[16,1024]{1,0:T(8,128)(4,1)S...) while((s32[]{:T(128)}, f32[16,1024,48]{1,2,0:T(8,128)}, ...), condition=%wide.region_15.16_spmd, body=%wide.region_14.15_spmd.sunk | while | flops 513900544 | bytes 21337212 | solution.py:102
  512.4 2.7 fusion.224
  625.5 2.7 fusion.224
  636.9 2.7 fusion.224
  662.5 7.9 copy.102
  670.3 7.8 copy.112
  678.2 7.8 copy.115
  686.0 5.5 copy.98
  691.5 4.2 fusion.114
  699.3 15.1 %fusion.110 = (bf16[1024,16,48]{2,1,0:T(8,128)(2,1)}, bf16[1024,16,48]{2,1,0:T(8,128)(2,1)}, bf16[1024,16,48]{2,1,0:T(8,128)(2,1)}) fusion(f32[16,1024,48]{2,0,1:T(8,128)} %copy.102, f32[64,16,48]{2,1,0:T(8,128)S(1)} %copy.110, pred[1024,16]{1,0:T(8,128)(4,1)} %copy-done.14, f32[64,16,48]{2,1,0:T(8,128)S(1)} %copy.113, f32[16,1024,48]{2,0,1:T(8,128)} %copy.112, ...), kind=kLoop, calls=%fused_computation.127 | loop fusion | flops 7077888 | bytes 14761984 | tf_op jit(solution)/shard_map/convert_element_type | solution.py:213
  714.4 5.5 copy.111
  719.9 4.2 fusion.132
  724.2 5.5 copy.114
  729.7 4.2 fusion.133
  734.0 4.4 copy.117
  738.4 4.2 fusion.134
  742.7 5.0 fusion.117
  750.9 2.7 fusion.118
  753.6 157.5 %all-reduce.3.cloned.1.call-done = (f32[768,768]{1,0:T(8,128)}, f32[768,768]{1,0:T(8,128)}, f32[768,768]{1,0:T(8,128)}, f32[768,768]{1,0:T(8,128)}) async-done(((f32[768,768]{1,0:T(8,128)}, f32[768,768]{1,0:T(8,128)}, f32[768,768]{1,0:T(8,128)}, f32[768,768]{1,0:T(8,128)}), (f32[768,768]{1,0:T(8,128)}, f32[768,768]{1,0:T(8,128)}, f32[768,768]{1,0:T(8,128)}, ...) | async-done | bytes 9437200 | tf_op jit(solution)/shard_map/psum | solution.py:232
  911.1 3.4 copy.189
  (565 shorter events, 447.1 us)
Async XLA Ops:
  7.2 23.6 %copy-start = (bf16[1,1024,768]{2,1,0:T(8,128)(2,1)S(1)}, bf16[1,1024,768]{2,1,0:T(8,128)(2,1)}, u32[]{:S(2)}) copy-start(bf16[1,1024,768]{2,1,0:T(8,128)(2,1)} %param.16) | copy-start | bytes 4718596
  36.1 6.4 copy-start.8
  36.1 29.0 %all-to-all-start.1 = ((bf16[8,128,768]{2,1,0:T(8,128)(2,1)}), bf16[8,128,768]{2,1,0:T(8,128)(2,1)}, u32[]{:S(2)}, u32[]{:S(2)}) async-start(bf16[8,128,768]{2,1,0:T(8,128)(2,1)} %broadcast_select_fusion), calls=%async_computation.1 | async-start | bytes 3145728 | tf_op jit(solution)/shard_map/all_to_all | solution.py:137
  40.5 255.1 %all-gather.2.cloned.1.call-start = ((), (), s32[]{:S(2)}) async-start(), calls=%async_computation.3 | async-start | bytes 1769472 | tf_op jit(solution)/shard_map/all_gather | solution.py:14
  41.9 0.6 copy-start.24
  63.1 0.5 copy-start.23
  63.7 1.4 copy-start.21
  64.4 281.8 %copy-start.14 = (pred[1024,16]{1,0:T(8,128)(4,1)}, pred[1024,16]{1,0:T(8,128)(4,1)S(1)}, u32[]{:S(2)}) copy-start(pred[1024,16]{1,0:T(8,128)(4,1)S(1)} %copy.94) | copy-start | bytes 49156
  71.5 3.3 copy-start.10
  132.4 563.3 %reduce-scatter.4.cloned.1.call-start = ((), (), s32[]{:S(2)}) async-start(), calls=%async_computation.4 | async-start | bytes 3538944
  135.9 3.2 copy-start.4
  139.0 3.2 copy-start.28
  139.0 5.3 copy-start.19
  139.0 5.3 copy-start.20
  144.3 142.7 %copy-start.16 = (bf16[64,16,48]{2,1,0:T(8,128)(2,1)S(1)}, bf16[64,16,48]{2,1,0:T(8,128)(2,1)}, u32[]{:S(2)}) copy-start(bf16[64,16,48]{2,1,0:T(8,128)(2,1)} %get-tuple-element.310) | copy-start | bytes 294916
  146.1 1.9 copy-start.2
  155.0 1.9 copy-start.2
  163.9 1.9 copy-start.2
  173.0 1.9 copy-start.2
  182.0 1.9 copy-start.2
  190.9 1.9 copy-start.2
  199.8 1.9 copy-start.2
  208.6 1.9 copy-start.2
  217.6 1.9 copy-start.2
  226.5 1.9 copy-start.2
  235.4 1.9 copy-start.2
  244.3 1.9 copy-start.2
  253.2 1.9 copy-start.2
  262.1 1.9 copy-start.2
  271.0 1.9 copy-start.2
  279.8 1.9 copy-start.2
  299.2 2.1 copy-start.18
  299.2 2.1 copy-start.26
  299.2 2.1 copy-start.27
  343.4 2.4 copy-start.17
  343.4 2.7 copy-start.25
  346.2 13.4 %copy-start.3 = (bf16[1024,16,48]{2,1,0:T(8,128)(2,1)S(1)}, bf16[1024,16,48]{2,1,0:T(8,128)(2,1)}, u32[]{:S(2)}) copy-start(bf16[1024,16,48]{2,1,0:T(8,128)(2,1)} %copy.100) | copy-start | bytes 4718596
  359.6 3.0 copy-start.22
  474.7 436.5 %all-reduce.3.cloned.1.call-start = ((), (), s32[]{:S(2)}) async-start(), calls=%async_computation.5 | async-start | bytes 18874368 | tf_op jit(solution)/shard_map/psum | solution.py:232
  686.0 5.5 copy-start.9
  714.4 5.5 copy-start.11
  742.7 5.0 copy-start.12
  742.7 5.0 copy-start.29
  747.7 1.5 copy-start.13
  747.7 1.7 copy-start.30
  749.4 1.5 copy-start.15
  911.1 3.4 copy-start.7
  914.5 2.5 copy-start.6
  917.0 2.5 copy-start.5
  917.0 3.9 copy-start.1
Sparse Core Ops, SparseCore 0:
  132.6 52.8 all-gather.1
  474.8 81.6 reduce-scatter.3
  742.8 168.2 all-reduce.2
where the time goes:
time: 942 us; the launch traced here: 928 us
  matrix products  454 us (48%)
  local copies, waits for them, and re-layouts  204 us (22%)
  waiting for transfers between devices  158 us (17%)
  other arithmetic  76.5 us (8%)
  between operations  15.1 us (2%)
  blocking collectives  13.8 us (1%)
    dot_general x224, matrix products, product(): jnp.einsum(pattern, left_side, right_side, preferred_element_type=jnp.flo...  413 us
    psum x1, waiting for transfers between devices, per_device(): lax.psum((grad_query, grad_key, grad_value, grad_outproj), ('seq', 'rep'))  158 us
    while x9, local copies, waits for them, and re-layouts, heads_map(): lax.map(lambda members: function(*members, pieces, scaling), transposed)  35.9 us
    while x32, local copies, waits for them, and re-layouts  30.8 us
    convert_element_type x6, local copies, waits for them, and re-layouts, sparse_rows(): dense.astype(jnp.float32)  30.7 us
    dot_general x8, matrix products, project(): return jnp.dot(left_side, right_side, preferred_element_type=jnp.float32)  24 us
  transfers between devices with their start and end apart: 4, of which 1 were waited for; matrix products, arithmetic and copies ran while one was open for 41% of the time, Pallas kernels for 0%

commit v1 on v0

--- a/solution.py
+++ b/solution.py
@@ -229,7 +229,7 @@
     grad_query = jnp.einsum("td,te->de", embedded, query_grad, preferred_element_type=jnp.float32)
     grad_key = jnp.einsum("td,te->de", embedded, key_grad, preferred_element_type=jnp.float32)
     grad_value = jnp.einsum("td,te->de", embedded, value_grad, preferred_element_type=jnp.float32)
-    summed = lax.psum((grad_query, grad_key, grad_value, grad_outproj), ("seq", "rep"))
+    summed = lax.psum(lax.psum((grad_query, grad_key, grad_value, grad_outproj), "seq"), "rep")
     return (encoded[None], embed_grad[None], summed[0], summed[1], summed[2], summed[3])
 
 

time: 942 us -> 1310 us (1.39)
  waiting for transfers between devices: 158 us -> 524 us
    psum x1 -> x2, waiting for transfers between devices: 158 us -> 524 us  [the longest x1 387 us: per_device(): lax.psum((grad_query, grad_key, grad_value, grad_outproj), 'seq')]
  transfers between devices with their start and end apart: 4 -> 5, of which waited for: 1 -> 2; matrix products, arithmetic and copies ran while one was open for 41% -> 30% of each run, Pallas kernels for 0% -> 0%
where the time goes in v1:
time: 1310 us; the launch traced here: 1290 us
  waiting for transfers between devices  524 us (40%)
  matrix products  453 us (35%)
  local copies, waits for them, and re-layouts  204 us (16%)
  other arithmetic  76.5 us (6%)
  between operations  15.1 us (1%)
  blocking collectives  13.8 us (1%)
    dot_general x224, matrix products, product(): jnp.einsum(pattern, left_side, right_side, preferred_element_type=jnp.flo...  413 us
    psum x1, waiting for transfers between devices, per_device(): lax.psum((grad_query, grad_key, grad_value, grad_outproj), 'seq')  387 us
    psum x1, waiting for transfers between devices, per_device(): lax.psum(lax.psum((grad_query, grad_key, grad_value, grad_outproj), 'seq'...  137 us
    while x9, local copies, waits for them, and re-layouts, heads_map(): lax.map(lambda members: function(*members, pieces, scaling), transposed)  35.9 us
    while x32, local copies, waits for them, and re-layouts  31 us
    convert_element_type x6, local copies, waits for them, and re-layouts, sparse_rows(): dense.astype(jnp.float32)  30.7 us
  transfers between devices with their start and end apart: 5, of which 2 were waited for; matrix products, arithmetic and copies ran while one was open for 30% of the time, Pallas kernels for 0%

profile of v1, /device:TPU:1, one launch (start us, length us, event | category | flops | bytes accessed | tf_op | source)
XLA Modules:
  0.0 1294.0 jit_solution(15999842829668564605)
XLA Ops:
  8.0 4.4 sort.17
  12.4 4.5 gather_fusion
  16.9 13.8 %all_to_all.14 = s32[8,1,128]{2,1,0:T(1,128)S(1)} all-to-all(s32[8,1,128]{2,1,0:T(1,128)S(1)} %bitcast.386), channel_id=1, replica_groups=mesh['seq'=8,'rep'=16] {'seq'}, dimensions={0} | all-to-all | bytes 8192 | tf_op jit(solution)/shard_map/all_to_all | solution.py:135
  30.7 4.0 gather_fusion.1
  36.1 4.4 all-to-all-start.1
  42.5 2.7 multiply_convert_fusion.2
  47.3 4.8 copy.100
  52.1 3.2 copy.99
  55.2 7.8 reshape.434
  65.1 6.4 scatter_custom_fusion
  71.5 3.3 convolution_convert_fusion.2
  76.8 7.8 reshape.431
  84.6 3.2 convolution_convert_fusion.1
  90.0 7.8 reshape.432
  97.8 4.3 convolution_convert_fusion
  102.1 3.1 copy.87
  105.2 7.8 reshape.433
  113.0 14.1 %select_reduce_fusion = (bf16[64,16,48]{2,1,0:T(8,128)(2,1)S(1)}, bf16[64,16,48]{2,1,0:T(8,128)(2,1)}, bf16[64,16,48]{2,1,0:T(8,128)(2,1)}, bf16[64,16,48]{2,1,0:T(8,128)(2,1)}) fusion(f32[64,16,16,48]{3,2,1,0:T(8,128)} %reshape.434, pred[16,16]{1,0:T(8,128)(4,1)} %copy-done.23, f32[64,16,16,48]{3,2,1,0:T(8,128)} %reshape.432, ...), kind=kLoop, calls=%fused_computation.133 | loop fusion | flops 6094848 | bytes 12976384 | tf_op jit(solution)/shard_map/reduce_sum | solution.py:38
  132.7 3.2 copy.80
  135.9 3.2 copy.81
  139.1 3.1 copy.82
  144.3 142.8 %while.56 = (s32[]{:T(128)}, f32[16,1024,48]{1,2,0:T(8,128)}, f32[16,1024]{1,0:T(8,128)S(1)}, f32[16,1024]{1,0:T(8,128)S(1)}, pred[16,1024]{1,0:T(8,128)(4,1)S(1...) while((s32[]{:T(128)}, f32[16,1024,48]{1,2,0:T(8,128)}, ...), condition=%wide.region_5.6_spmd, body=%wide.region_2.5_spmd.sunk | while | flops 212858880 | bytes 30383244 | solution.py:102
  149.1 4.0 fusion.204
  158.0 4.0 fusion.204
  166.9 4.2 fusion.204
  176.1 4.0 fusion.204
  185.0 4.0 fusion.204
  193.9 4.0 fusion.204
  202.8 4.0 fusion.204
  211.7 4.0 fusion.204
  220.6 4.0 fusion.204
  229.5 4.0 fusion.204
  238.4 4.0 fusion.204
  247.4 4.0 fusion.204
  256.3 4.0 fusion.204
  265.2 4.0 fusion.204
  274.1 4.0 fusion.204
  283.0 4.0 fusion.204
  287.2 7.9 copy.83
  301.4 42.2 %while.57 = (s32[]{:T(128)}, f32[16,64,48]{1,2,0:T(8,128)S(1)}, f32[16,64]{1,0:T(8,128)S(1)}, f32[16,64]{1,0:T(8,128)S(1)}, pred[16,512]{1,0:T(8,128)(4,1)S(1)},...) while((s32[]{:T(128)}, f32[16,64,48]{1,2,0:T(8,128)S(1)}, ...), condition=%wide.region_12.13_spmd, body=%wide.region_9.12_spmd.sunk | while | flops 6520706 | bytes 702321 | solution.py:102
  346.3 13.4 %multiply_convert_fusion.1 = (bf16[1024,16,48]{2,1,0:T(8,128)(2,1)}, f32[1024,16,48]{2,1,0:T(8,128)S(1)}) fusion(f32[1024]{0:T(1024)S(1)} %copy-done.25, f32[1024,16]{1,0:T(8,128)} %copy.97, f32[1024,16]{1,0:T(8,128)S(1)} %copy.96, f32[64,16,48]{2,1,0:T(8,128)S(1)} %copy.95, pred[1024,16]{1,0:T(8,128)(4,1)S(1)} %copy.94, f32[1024,16]{1,0:T(8,128)S(1)} %copy.93, ...), kind=kLoop, calls=%fused_computation.135 | loop fusion | flops 5505024 | bytes 8278016 | tf_op jit(solution)/shard_map/convert_element_type | solution.py:172
  363.1 103.9 %while.59 = (s32[]{:T(128)}, f32[16,64,48]{1,2,0:T(8,128)S(1)}, f32[16,512,48]{1,2,0:T(8,128)}, f32[16,512,48]{1,2,0:T(8,128)}, pred[16,512]{1,0:T(8,128)(4,1)S(...) while((s32[]{:T(128)}, f32[16,64,48]{1,2,0:T(8,128)S(1)}, ...), condition=%wide.region_20.21_spmd, body=%wide.region_19.20_spmd.sunk | while | flops 15985666 | bytes 1278077 | solution.py:102
  467.0 3.9 pad_maximum_fusion
  470.8 3.9 copy.119
  481.1 181.1 %while.58 = (s32[]{:T(128)}, f32[16,1024,48]{1,2,0:T(8,128)}, f32[16,1024,48]{1,2,0:T(8,128)}, f32[16,1024,48]{1,2,0:T(8,128)}, pred[16,1024]{1,0:T(8,128)(4,1)S...) while((s32[]{:T(128)}, f32[16,1024,48]{1,2,0:T(8,128)}, ...), condition=%wide.region_15.16_spmd, body=%wide.region_14.15_spmd.sunk | while | flops 513900544 | bytes 21337212 | solution.py:102
  557.8 2.7 fusion.224
  591.7 2.7 fusion.224
  636.9 2.7 fusion.224
  662.5 7.9 copy.102
  670.4 7.8 copy.112
  678.2 7.9 copy.115
  686.1 5.5 copy.98
  691.6 4.2 fusion.114
  699.3 15.1 %fusion.110 = (bf16[1024,16,48]{2,1,0:T(8,128)(2,1)}, bf16[1024,16,48]{2,1,0:T(8,128)(2,1)}, bf16[1024,16,48]{2,1,0:T(8,128)(2,1)}) fusion(f32[16,1024,48]{2,0,1:T(8,128)} %copy.102, f32[64,16,48]{2,1,0:T(8,128)S(1)} %copy.110, pred[1024,16]{1,0:T(8,128)(4,1)} %copy-done.14, f32[64,16,48]{2,1,0:T(8,128)S(1)} %copy.113, f32[16,1024,48]{2,0,1:T(8,128)} %copy.112, ...), kind=kLoop, calls=%fused_computation.127 | loop fusion | flops 7077888 | bytes 14761984 | tf_op jit(solution)/shard_map/convert_element_type | solution.py:213
  714.5 5.5 copy.111
  720.0 4.2 fusion.132
  724.2 5.5 copy.114
  729.7 4.2 fusion.133
  734.0 4.4 copy.117
  738.4 4.2 fusion.134
  742.8 387.0 %all-reduce.7.cloned.1.call-done = (f32[768,768]{1,0:T(8,128)}, f32[768,768]{1,0:T(8,128)}, f32[768,768]{1,0:T(8,128)}, f32[768,768]{1,0:T(8,128)}) async-done(((f32[768,768]{1,0:T(8,128)}, f32[768,768]{1,0:T(8,128)}, f32[768,768]{1,0:T(8,128)}, f32[768,768]{1,0:T(8,128)}), (f32[768,768]{1,0:T(8,128)}, f32[768,768]{1,0:T(8,128)}, f32[768,768]{1,0:T(8,128)}, ...) | async-done | bytes 9437200 | tf_op jit(solution)/shard_map/psum | solution.py:232
  1129.8 5.0 fusion.117
  1140.7 136.7 %all-reduce.5.cloned.1.call-done = (f32[768,768]{1,0:T(8,128)}, f32[768,768]{1,0:T(8,128)}, f32[768,768]{1,0:T(8,128)}, f32[768,768]{1,0:T(8,128)}) async-done(((f32[768,768]{1,0:T(8,128)}, f32[768,768]{1,0:T(8,128)}, f32[768,768]{1,0:T(8,128)}, f32[768,768]{1,0:T(8,128)}), (f32[768,768]{1,0:T(8,128)}, f32[768,768]{1,0:T(8,128)}, f32[768,768]{1,0:T(8,128)}, ...) | async-done | bytes 9437200 | tf_op jit(solution)/shard_map/psum | solution.py:232
  1277.4 3.4 copy.193
  (568 shorter events, 449.8 us)
Async XLA Ops:
  7.2 23.6 %copy-start = (bf16[1,1024,768]{2,1,0:T(8,128)(2,1)S(1)}, bf16[1,1024,768]{2,1,0:T(8,128)(2,1)}, u32[]{:S(2)}) copy-start(bf16[1,1024,768]{2,1,0:T(8,128)(2,1)} %param.16) | copy-start | bytes 4718596
  36.1 6.4 copy-start.8
  36.1 29.0 %all-to-all-start.1 = ((bf16[8,128,768]{2,1,0:T(8,128)(2,1)}), bf16[8,128,768]{2,1,0:T(8,128)(2,1)}, u32[]{:S(2)}, u32[]{:S(2)}) async-start(bf16[8,128,768]{2,1,0:T(8,128)(2,1)} %broadcast_select_fusion), calls=%async_computation.1 | async-start | bytes 3145728 | tf_op jit(solution)/shard_map/all_to_all | solution.py:137
  40.5 255.2 %all-gather.2.cloned.1.call-start = ((), (), s32[]{:S(2)}) async-start(), calls=%async_computation.3 | async-start | bytes 1769472 | tf_op jit(solution)/shard_map/all_gather | solution.py:14
  41.9 0.6 copy-start.24
  63.1 0.6 copy-start.23
  63.8 1.4 copy-start.21
  64.4 281.9 %copy-start.14 = (pred[1024,16]{1,0:T(8,128)(4,1)}, pred[1024,16]{1,0:T(8,128)(4,1)S(1)}, u32[]{:S(2)}) copy-start(pred[1024,16]{1,0:T(8,128)(4,1)S(1)} %copy.94) | copy-start | bytes 49156
  71.5 3.3 copy-start.10
  132.4 563.3 %reduce-scatter.4.cloned.1.call-start = ((), (), s32[]{:S(2)}) async-start(), calls=%async_computation.4 | async-start | bytes 3538944
  135.9 3.2 copy-start.4
  139.0 3.2 copy-start.28
  139.0 5.2 copy-start.19
  139.0 5.2 copy-start.20
  144.3 142.8 %copy-start.16 = (bf16[64,16,48]{2,1,0:T(8,128)(2,1)S(1)}, bf16[64,16,48]{2,1,0:T(8,128)(2,1)}, u32[]{:S(2)}) copy-start(bf16[64,16,48]{2,1,0:T(8,128)(2,1)} %get-tuple-element.310) | copy-start | bytes 294916
  146.1 1.9 copy-start.2
  155.0 1.9 copy-start.2
  163.9 1.9 copy-start.2
  173.1 1.9 copy-start.2
  182.0 1.9 copy-start.2
  190.9 1.9 copy-start.2
  199.8 1.9 copy-start.2
  208.7 1.9 copy-start.2
  217.6 1.9 copy-start.2
  226.6 1.9 copy-start.2
  235.5 1.9 copy-start.2
  244.4 1.9 copy-start.2
  253.3 1.9 copy-start.2
  262.2 1.9 copy-start.2
  271.1 1.9 copy-start.2
  280.0 1.9 copy-start.2
  299.3 2.1 copy-start.18
  299.3 2.1 copy-start.26
  299.3 2.1 copy-start.27
  343.6 2.4 copy-start.17
  343.6 2.7 copy-start.25
  346.3 13.4 %copy-start.3 = (bf16[1024,16,48]{2,1,0:T(8,128)(2,1)S(1)}, bf16[1024,16,48]{2,1,0:T(8,128)(2,1)}, u32[]{:S(2)}) copy-start(bf16[1024,16,48]{2,1,0:T(8,128)(2,1)} %copy.100) | copy-start | bytes 4718596
  359.7 3.0 copy-start.22
  474.8 655.0 %all-reduce.7.cloned.1.call-start = ((), (), s32[]{:S(2)}) async-start(), calls=%async_computation.6 | async-start | bytes 18874368 | tf_op jit(solution)/shard_map/psum | solution.py:232
  686.1 5.5 copy-start.9
  714.5 5.5 copy-start.11
  742.7 534.7 %all-reduce.5.cloned.1.call-start = ((), (), s32[]{:S(2)}) async-start(), calls=%async_computation.5 | async-start | bytes 18874368 | tf_op jit(solution)/shard_map/psum | solution.py:232
  1129.8 5.0 copy-start.12
  1129.8 5.0 copy-start.29
  1134.8 1.5 copy-start.13
  1134.8 1.7 copy-start.30
  1136.6 1.5 copy-start.15
  1277.4 3.4 copy-start.7
  1280.8 2.5 copy-start.6
  1283.3 2.5 copy-start.5
  1283.3 3.9 copy-start.1
Sparse Core Ops, SparseCore 0:
  132.6 52.8 all-gather.1
  474.9 81.6 reduce-scatter.3
  742.8 386.9 all-reduce.6
  1132.4 144.9 all-reduce.4
